TPU v7x, 512 devices: a whole 4x4x16 slice. The times are simulated.
512 devices in a mesh: row: 32 (over z, core), col: 16 (over x, y).
Axes of the slice: x: 4, y: 4, z: 16, core: 2. Of those that a mesh axis runs over, the one named last changes fastest.
Arguments:
- source: bfloat16 [32768, 256], P(('row', 'col')), may hold values from -1.5 to 1.5
- target: bfloat16 [32768, 256], P(('col', 'row')), may hold values from -1.5 to 1.5
- g_init: float32 [32768], P('col'), may hold values from -25 to 25
- pairs: int32 [64, 64], P('row', 'col'), may hold values from 0 to 1, as said below
Outputs:
- f_out: float32 [32768], P('row')
- g_out: float32 [32768], P('col')
Inputs may be any that keep to these rules, and one draw needn't show every extreme that they name: Values are 0 or 1; every block of source cells and every block of target cells has at least one kept pair; the share of kept pairs differs between devices' tiles.
All inputs are finite; a program needn't handle non-finite values.
Results may differ from a plain program's by a relative error of at most 0.0003.
Values may be sent and summed in bfloat16 or wider, within the bound.
No kernel may reach another device: no remote copies, remote signals or barrier semaphores. Data moves between devices by JAX's collectives and lax.ppermute only.
A program may use at most 64 MiB of HBM per device.

v0:
```python
import jax
import jax.numpy as jnp
from jax import lax
from jax.sharding import Mesh
from jax.sharding import PartitionSpec as P

BLK = 512
ROW = ("row_0", "row_1")
ROW_COL = ("row_0", "row_1", "col")
COL_ROW = ("col", "row_0", "row_1")


EPSILON = 0.1
VERY_LOW = -1e30


def from_everyone(shard, axis):
    peers = lax.axis_size(axis)
    return lax.all_to_all(
        jnp.broadcast_to(shard[None], (peers, *shard.shape)), axis, 0, 0, tiled=True
    )


def gathered_once(shard, axis):
    leaves = jax.tree.leaves(shard)
    order = sorted(range(len(leaves)), key=lambda k: -leaves[k].size)
    width = (1, *leaves[order[0]].shape)[-1]
    lines = [
        jnp.pad(leaves[k].reshape(-1), (0, -leaves[k].size % width)).reshape(-1, width)
        for k in order
    ]
    both, at, found = (from_everyone(jnp.concatenate(lines), axis), 0, {})
    for k, line in zip(order, lines):
        share = both[:, at : at + len(line)].reshape(len(both), -1)
        found[k] = share[:, : leaves[k].size].reshape(-1, *leaves[k].shape)
        at += len(line)
    numbers = iter(range(len(leaves)))
    return jax.tree.map(lambda _: found[next(numbers)], shard)


def joined_by_halves(pieces, combine):
    while len(jax.tree.leaves(pieces)[0]) > 1:
        pieces = jax.vmap(combine)(
            *(jax.tree.map(lambda part: part[side::2], pieces) for side in (0, 1))
        )
    return jax.tree.map(lambda part: part[0], pieces)


def joined_all(shard, axis, combine):
    pieces = gathered_once(shard, axis)
    return joined_by_halves(pieces, combine)


def gathered_once_2(shard, axis):
    leaves = jax.tree.leaves(shard)
    order = sorted(range(len(leaves)), key=lambda k: -leaves[k].size)
    width = (1, *leaves[order[0]].shape)[-1]
    lines = [
        jnp.pad(leaves[k].reshape(-1), (0, -leaves[k].size % width)).reshape(-1, width)
        for k in order
    ]
    both, at, found = (lax.all_gather(jnp.concatenate(lines), axis), 0, {})
    for k, line in zip(order, lines):
        share = both[:, at : at + len(line)].reshape(len(both), -1)
        found[k] = share[:, : leaves[k].size].reshape(-1, *leaves[k].shape)
        at += len(line)
    numbers = iter(range(len(leaves)))
    return jax.tree.map(lambda _: found[next(numbers)], shard)


def gathered_by_type(shard, axis):
    leaves, found = (jax.tree.leaves(shard), {})
    for initial, a in enumerate(leaves):
        if initial not in found:
            alike = [k for k, b in enumerate(leaves) if b.dtype == a.dtype]
            got = (
                gathered_once_2([leaves[k] for k in alike], axis)
                if len(alike) > 1
                else [lax.all_gather(a, axis)]
            )
            for k, b in zip(alike, got):
                found[k] = b
    numbers = iter(range(len(leaves)))
    return jax.tree.map(lambda _: found[next(numbers)], shard)


def combined_by_axis(shard, axes, combine):
    for axis in axes:
        pieces = gathered_by_type(shard, axis)
        shard = jax.tree.map(lambda part: part[0], pieces)
        for k in range(1, lax.axis_size(axis)):
            shard = combine(shard, jax.tree.map(lambda part: part[k], pieces))
    return shard


def laid_out(tiles, dim):
    shape = list(tiles.shape[1:])
    shape[dim] *= tiles.shape[0]
    return jnp.moveaxis(tiles, 0, dim).reshape(shape)


def gathered_copies(shard, axis, dim):
    return laid_out(from_everyone(shard, axis), dim)


def stacked_from(shard, axes, order):
    tiles = shard
    for k in order:
        tiles = lax.all_gather(tiles, axes[k])
    done = order[::-1]
    back = [done.index(k) for k in range(len(axes))]
    tiles = tiles.transpose(*back, *range(len(axes), tiles.ndim))
    return tiles.reshape(-1, *shard.shape)


def gather_axes(shard, axes, order, dim):
    return laid_out(stacked_from(shard, axes, order), dim)


def block_cost(rows, cols, left, right):
    inner = lax.dot_general(
        rows, cols, (((1,), (1,)), ((), ())), preferred_element_type=jnp.float32
    )
    return left[:, None] + right[None, :] - inner


def combine(first, second):
    peak = jnp.maximum(first[0], second[0])
    total = first[1] * jnp.exp(first[0] - peak) + second[1] * jnp.exp(second[0] - peak)
    return (peak, total)


def row_partials(sources, targets, left, right, g_local, pairs, log_nt):
    row_blocks, col_blocks = pairs.shape
    peaks = []
    totals = []
    for row_block in range(row_blocks):
        rows = sources[row_block * BLK : (row_block + 1) * BLK]
        keep = jnp.repeat(pairs[row_block] > 0, BLK)
        cost = block_cost(rows, targets, left[row_block * BLK : (row_block + 1) * BLK], right)
        score = (g_local[None, :] - cost) / EPSILON - log_nt
        peak = jnp.max(jnp.where(keep[None, :], score, VERY_LOW), axis=1)
        peaks.append(peak)
        totals.append(
            jnp.sum(jnp.where(keep[None, :], jnp.exp(score - peak[:, None]), 0.0), axis=1)
        )
    return (jnp.concatenate(peaks), jnp.concatenate(totals))


def col_partials(sources, targets, left, right, f_local, pairs, log_ns):
    row_blocks, col_blocks = pairs.shape
    start = (
        jnp.full((targets.shape[0],), VERY_LOW, jnp.float32),
        jnp.zeros((targets.shape[0],), jnp.float32),
    )
    peak, total = start
    for row_block in range(row_blocks):
        rows = sources[row_block * BLK : (row_block + 1) * BLK]
        keep = jnp.repeat(pairs[row_block] > 0, BLK)
        cost = block_cost(rows, targets, left[row_block * BLK : (row_block + 1) * BLK], right)
        score = (
            f_local[row_block * BLK : (row_block + 1) * BLK][:, None] - cost
        ) / EPSILON - log_ns
        new_peak = jnp.maximum(peak, jnp.max(jnp.where(keep[None, :], score, VERY_LOW), axis=0))
        added = jnp.sum(jnp.where(keep[None, :], jnp.exp(score - new_peak[None, :]), 0.0), axis=0)
        total = total * jnp.exp(peak - new_peak) + added
        peak = new_peak
    return (peak, total)


def finish_rows(peak, total):
    peak, total = joined_all((peak, total), "col", combine)
    return -EPSILON * (peak + jnp.log(total))


def finish_cols(peak, total):
    peak, total = combined_by_axis((peak, total), ROW, combine)
    return -EPSILON * (peak + jnp.log(total))


def local(source, target, g_init, pairs):
    sources = gathered_copies(source, "col", 0)
    targets = gather_axes(target, ROW, (0, 1), 0)
    left = 0.5 * jnp.sum(jnp.square(sources.astype(jnp.float32)), axis=1)
    right = 0.5 * jnp.sum(jnp.square(targets.astype(jnp.float32)), axis=1)
    log_nt = jnp.log(jnp.float32(lax.axis_size("col") * targets.shape[0]))
    log_ns = jnp.log(jnp.float32(lax.axis_size(ROW) * sources.shape[0]))
    peak, total = row_partials(sources, targets, left, right, g_init, pairs, log_nt)
    f_local = finish_rows(peak, total)
    peak, total = col_partials(sources, targets, left, right, f_local, pairs, log_ns)
    g_local = finish_cols(peak, total)
    return (f_local, g_local)


def solution(mesh):
    finer = Mesh(mesh.devices.reshape(16, 2, mesh.shape["col"]), ("row_0", "row_1", "col"))
    placed = (P(ROW_COL, None), P(COL_ROW, None), P("col"), P(ROW, "col"))
    return jax.shard_map(
        local, mesh=finer, in_specs=placed, out_specs=(P(ROW), P("col")), check_vma=False
    )
```

profile of v0, /device:TPU:1, one launch (start us, length us, event | category | flops | bytes accessed | tf_op | source)
XLA Modules:
  0.0 152.3 jit_solution(10035017804245041605)
XLA Ops:
  7.2 1.6 %broadcast_in_dim.95 = bf16[16,64,256]{2,1,0:T(8,128)(2,1)} broadcast(bf16[64,256]{1,0:T(8,128)(2,1)} %param.4), dimensions={1,2} | broadcast | bytes 557056 | tf_op jit(solution)/shard_map/broadcast_in_dim | solution.py:20
  8.8 7.6 %all-to-all-start = ((bf16[16,64,256]{2,1,0:T(8,128)(2,1)}), bf16[16,64,256]{2,1,0:T(8,128)(2,1)S(1)}, u32[]{:S(2)}, u32[]{:S(2)}) async-start(bf16[16,64,256]{2,1,0:T(8,128)(2,1)} %broadcast_in_dim.95), calls=%async_computation | async-start | bytes 1048576 | tf_op jit(solution)/shard_map/all_to_all | solution.py:19
  16.4 34.1 %all-gather = bf16[1024,256]{1,0:T(8,128)(2,1)} all-gather(bf16[64,256]{1,0:T(8,128)(2,1)} %param.5), channel_id=2, replica_groups=mesh['row_0'=16,'row_1'=2,'col'=16] {'row_0'}, dimensions={0}, use_global_device_ids=true | all-gather | bytes 557056 | tf_op jit(solution)/shard_map/all_gather | solution.py:109
  50.6 0.8 compare_bitcast_fusion
  51.3 0.1 broadcast_bitcast_fusion
  51.4 0.2 multiply_reduce_fusion.1
  51.7 0.1 slice.297
  51.9 23.0 %all-gather.8.cloned.1.call-done = bf16[32,64,256]{2,1,0:T(8,128)(2,1)} async-done(((bf16[16,64,256]{2,1,0:T(8,128)(2,1)}), bf16[32,64,256]{2,1,0:T(8,128)(2,1)}) %all-gather.8.cloned.1.call-update) | async-done | bytes 1048592 | tf_op jit(solution)/shard_map/all_gather | solution.py:109
  74.8 1.6 %multiply_reduce_fusion = f32[16,2,64]{2,0,1:T(8,128)S(1)} fusion(bf16[16,2,64,256]{3,2,0,1:T(8,128)(2,1)} %bitcast.368), kind=kLoop, calls=%fused_computation.14 | loop fusion | flops 1570816 | bytes 1056768 | tf_op jit(solution)/shard_map/reduce_sum | solution.py:185
  76.4 1.3 copy.16
  77.7 0.1 mul.379
  77.8 1.4 select_reduce_fusion.7
  79.2 2.9 %select_reduce_fusion.5 = (f32[512]{0:T(512)S(1)}, f32[512]{0:T(512)S(1)}, f32[512,2048]{1,0:T(8,128)S(1)}) fusion(f32[512,2048]{1,0:T(8,128)S(1)} %get-tuple-element.31, f32[512]{0:T(512)S(1)} %get-tuple-element.30, f32[2048]{0:T(1024)S(1)} %mul.379, f32[512]{0:T(512)S(1)} %slice.292, f32[2048]{0:T(1024)S(1)} %copy-done.4, ...), kind=kOutput, calls=%fused_computation.7 | convolution fusion | flops 552598528 | bytes 9730048 | tf_op jit(solution)/shard_map/dot_general | solution.py:121
  82.1 1.9 %copy-done = f32[512,2048]{1,0:T(8,128)} copy-done((f32[512,2048]{1,0:T(8,128)}, f32[512,2048]{1,0:T(8,128)S(1)}, u32[]{:S(2)}) %copy-start) | copy-done | bytes 4194328
  84.1 1.5 %select_reduce_fusion.4 = f32[512]{0:T(512)S(1)} fusion(f32[512,2048]{1,0:T(8,128)S(1)} %get-tuple-element.32, f32[512]{0:T(512)S(1)} %get-tuple-element.3, f32[512]{0:T(512)S(1)} %slice.297, f32[2048]{0:T(1024)S(1)} %mul.379, f32[2048]{0:T(1024)S(1)} %copy-done.4, pred[2048]{0:T(1024)(128)(4,1)S(1)} %bitcast.382), kind=kLoop, calls=%fused_computation.6 | loop fusion | flops 8388096 | bytes 4218880 | tf_op jit(solution)/shard_map/reduce_sum | solution.py:145
  85.7 12.1 %all_to_all.10 = f32[16,2,1024]{2,1,0:T(2,128)S(1)} all-to-all(f32[16,2,1024]{2,1,0:T(2,128)S(1)} %broadcast_in_dim.101), channel_id=1, replica_groups=mesh['row_0'=16,'row_1'=2,'col'=16] {'col'}, dimensions={0} | all-to-all | bytes 262144 | tf_op jit(solution)/shard_map/all_to_all | solution.py:19
  97.8 0.1 fusion.67
  98.4 3.8 %select_reduce_fusion.3 = f32[2048]{0:T(1024)S(1)} fusion(f32[512,2048]{1,0:T(8,128)} %copy-done.2, f32[512]{0:T(512)S(1)} %bitcast.397, f32[2048]{0:T(1024)S(1)} %mul.379, f32[512]{0:T(512)S(1)} %slice.292, pred[2048]{0:T(1024)(128)(4,1)S(1)} %bitcast.393), kind=kLoop, calls=%fused_computation.4 | loop fusion | flops 7337984 | bytes 4216832 | tf_op jit(solution)/shard_map/reduce_max | solution.py:164
  102.2 5.3 %select_reduce_fusion.1 = (f32[2048]{0:T(1024)S(1)}, f32[2048]{0:T(1024)S(1)}) fusion(f32[512,2048]{1,0:T(8,128)} %copy-done.2, f32[2048]{0:T(1024)S(1)} %broadcast_maximum_fusion, f32[512]{0:T(512)S(1)} %bitcast.398, f32[2048]{0:T(1024)S(1)} %mul.379, f32[512]{0:T(512)S(1)} %slice.292, pred[2048]{0:T(1024)(128)(4,1)S(1)} %bitcast.394, ...), kind=kLoop, calls=%fused_computation.1 | loop fusion | flops 15724544 | bytes 8433664 | tf_op jit(solution)/shard_map/reduce_sum | solution.py:165
  107.6 2.0 %select_reduce_fusion = f32[2048]{0:T(1024)S(1)} fusion(f32[512,2048]{1,0:T(8,128)S(1)} %copy-done.1, f32[2048]{0:T(1024)S(1)} %fusion.64, f32[512]{0:T(512)S(1)} %bitcast.396, f32[512]{0:T(512)S(1)} %slice.297, f32[2048]{0:T(1024)S(1)} %mul.379, pred[2048]{0:T(1024)(128)(4,1)S(1)} %bitcast.384), kind=kLoop, calls=%fused_computation | loop fusion | flops 8386560 | bytes 4225024 | tf_op jit(solution)/shard_map/reduce_sum | solution.py:165
  109.6 24.7 %all-gather.4 = f32[16,2,2048]{2,1,0:T(2,128)S(1)} all-gather(f32[1,2,2048]{2,1,0:T(2,128)S(1)} %maximum_bitcast_fusion), channel_id=4, replica_groups=mesh['row_0'=16,'row_1'=2,'col'=16] {'row_0'}, dimensions={0}, use_global_device_ids=true | all-gather | bytes 278528 | tf_op jit(solution)/shard_map/all_gather | solution.py:62
  134.3 0.4 fusion.1
  134.8 10.0 %all-gather.5 = f32[2,2,2048]{2,1,0:T(2,128)S(1)} all-gather(f32[1,2,2048]{2,1,0:T(2,128)S(1)} %maximum_bitcast_fusion.1), channel_id=5, replica_groups=mesh['row_0'=16,'row_1'=2,'col'=16] {'row_1'}, dimensions={0}, use_global_device_ids=true | all-gather | bytes 49152 | tf_op jit(solution)/shard_map/all_gather | solution.py:62
  144.8 0.6 add_multiply_fusion
  (49 shorter events, 0.8 us)
Async XLA Ops:
  7.2 70.7 %copy-start.4 = (f32[2048]{0:T(1024)S(1)}, f32[2048]{0:T(1024)}, u32[]{:S(2)}) copy-start(f32[2048]{0:T(1024)} %param.6) | copy-start | bytes 24580
  8.8 42.6 %all-to-all-start = ((bf16[16,64,256]{2,1,0:T(8,128)(2,1)}), bf16[16,64,256]{2,1,0:T(8,128)(2,1)S(1)}, u32[]{:S(2)}, u32[]{:S(2)}) async-start(bf16[16,64,256]{2,1,0:T(8,128)(2,1)} %broadcast_in_dim.95), calls=%async_computation | async-start | bytes 1048576 | tf_op jit(solution)/shard_map/all_to_all | solution.py:19
  16.4 58.5 %all-gather.8.cloned.1.call-start = ((), (), s32[]{:S(2)}) async-start(), calls=%async_computation.2 | async-start | bytes 1572864 | tf_op jit(solution)/shard_map/all_gather | solution.py:109
  79.2 2.9 %copy-start.2 = (f32[512,2048]{1,0:T(8,128)}, f32[512,2048]{1,0:T(8,128)S(1)}, u32[]{:S(2)}) copy-start(f32[512,2048]{1,0:T(8,128)S(1)} %get-tuple-element.31) | copy-start | bytes 12582916
  82.1 2.0 %copy-start = (f32[512,2048]{1,0:T(8,128)}, f32[512,2048]{1,0:T(8,128)S(1)}, u32[]{:S(2)}) copy-start(f32[512,2048]{1,0:T(8,128)S(1)} %get-tuple-element.32) | copy-start | bytes 12582916
  98.3 3.9 %copy-start.1 = (f32[512,2048]{1,0:T(8,128)S(1)}, f32[512,2048]{1,0:T(8,128)}, u32[]{:S(2)}) copy-start(f32[512,2048]{1,0:T(8,128)} %copy-done) | copy-start | bytes 12582916
  98.3 9.2 %copy-start.3 = (f32[1,1024]{1,0:T(1,128)}, f32[1,1024]{1,0:T(1,128)S(1)}, u32[]{:S(2)}) copy-start(f32[1,1024]{1,0:T(1,128)S(1)} %add_multiply_fusion.1) | copy-start | bytes 12292
Sparse Core Ops, SparseCore 0:
  50.7 24.1 all-gather.7
where the time goes:
time: 153 us; the launch traced here: 152 us
  blocking collectives  80.9 us (53%)
  waiting for transfers between devices  23 us (15%)
  other arithmetic  16.5 us (11%)
  between operations  14.3 us (9%)
  starting transfers between devices  7.61 us (5%)
  local copies, waits for them, and re-layouts  5.74 us (4%)
  matrix products  4.26 us (3%)
    all_gather x2, blocking collectives, gathered_once_2(): both, at, found = (lax.all_gather(jnp.concatenate(lines), axis), 0, {})  34.7 us
    all_gather x1, blocking collectives, stacked_from(): tiles = lax.all_gather(tiles, axes[k])  34.1 us
    all_gather x1, waiting for transfers between devices, stacked_from(): tiles = lax.all_gather(tiles, axes[k])  23 us
    all_to_all x1, blocking collectives, from_everyone(): lax.all_to_all(jnp.broadcast_to(shard[None], (peers, *shard.shape)), axis...  12.1 us
    all_to_all x1, starting transfers between devices, from_everyone(): lax.all_to_all(jnp.broadcast_to(shard[None], (peers, *shard.shape)), axis...  7.57 us
    reduce_sum x2, other arithmetic, col_partials(): jnp.sum(jnp.where(keep[None, :], jnp.exp(score - new_peak[None, :]), 0.0)...  7.31 us
    dot_general x2, matrix products, block_cost(): lax.dot_general(rows, cols, (((1,), (1,)), ((), ())), preferred_element_t...  4.26 us
    reduce_max x1, other arithmetic, col_partials(): jnp.max(jnp.where(keep[None, :], score, VERY_LOW), axis=0)  3.82 us
  transfers between devices with their start and end apart: 2, of which 1 were waited for; matrix products, arithmetic and copies ran while one was open for 1% of the time, Pallas kernels for 0%

commit v1 on v0

v1 whole, which is shorter than its diff:
```python
import math

import jax
import jax.numpy as jnp
from jax import lax
from jax.experimental import pallas as pl
from jax.experimental.pallas import tpu as pltpu
from jax.sharding import Mesh
from jax.sharding import PartitionSpec as P


BLK = 512
DL = 256
LANES = 128
EPSILON = 0.1
VERY_LOW = -1e30
SCALE = math.log2(math.e) / EPSILON
UNSCALE = EPSILON * math.log(2.0)
ROW = ("z", "core")
VMEM = pl.BlockSpec(memory_space=pltpu.VMEM)
SMEM = pl.BlockSpec(memory_space=pltpu.SMEM)
f32 = jnp.float32


def half_norms(x):
    x = x.astype(f32)
    return 0.5 * jnp.sum(x * x, axis=1, keepdims=True)


def turned(x):
    rows = x.shape[0]
    if rows < LANES:
        x = jnp.concatenate([x, jnp.zeros((LANES - rows, LANES), f32)], axis=0)
    return x.T


def joined(parts):
    peak = jnp.max(parts, axis=0)
    return peak + jnp.log2(jnp.sum(jnp.exp2(parts - peak[None]), axis=0))


def reduced_over(kept, many, few, left, right, bias_ref, score_ref, peak_ref, total_ref):
    peak_ref[...] = jnp.full(peak_ref.shape, VERY_LOW, f32)
    total_ref[...] = jnp.zeros(total_ref.shape, f32)
    per = BLK // LANES

    def scores(step, _):
        a, b = step // few, step % few

        @pl.when(kept(a, b))
        def _():
            y = right(b)
            peak = peak_ref[b]
            for q in range(per):
                x = left(a * per + q)
                inner = lax.dot_general(
                    x, y, (((1,), (1,)), ((), ())), preferred_element_type=f32
                )
                bias = bias_ref[a * per + q]
                s = inner * SCALE + jnp.concatenate([bias] * (BLK // LANES), axis=1)
                score_ref[step, q] = s
                peak = jnp.maximum(peak, jnp.max(s.reshape(LANES // 8, 8, BLK), axis=0))
            peak_ref[b] = peak

        return 0

    def sums(step, _):
        a, b = step // few, step % few

        @pl.when(kept(a, b))
        def _():
            peak = peak_ref[b]
            total = total_ref[b]
            for q in range(per):
                s = score_ref[step, q].reshape(LANES // 8, 8, BLK)
                total = total + jnp.sum(jnp.exp2(s - peak[None]), axis=0)
            total_ref[b] = total

        return 0

    lax.fori_loop(0, many * few, scores, 0)
    lax.fori_loop(0, many * few, sums, 0)
    lines = []
    for b in range(few):
        peak, total = peak_ref[b], total_ref[b]
        top = jnp.max(peak, axis=0, keepdims=True)
        total = jnp.sum(total * jnp.exp2(peak - top), axis=0, keepdims=True)
        line = jnp.where(total > 0.0, top + jnp.log2(total), VERY_LOW)
        lines += [line[:, k * LANES : (k + 1) * LANES] for k in range(per)]
    return lines


def row_kernel(pairs_ref, core_ref, src_ref, own_ref, other_ref, g_ref,
               out_ref, tgt_ref, right_ref,
               line_ref, bias_ref, score_ref, peak_ref, total_ref):
    core = core_ref[0]
    tgt_ref[:, core] = own_ref[...]
    tgt_ref[:, 1 - core] = other_ref[...]
    lines = tgt_ref.shape[0]
    g = turned(g_ref[...])
    lane = lax.broadcasted_iota(jnp.int32, (LANES, LANES), 1)
    norms = jnp.zeros((LANES, LANES), f32)
    for k in range(lines):
        n = half_norms(tgt_ref[k].reshape(LANES, DL))
        norms = jnp.where(lane == k, n, norms)
        bias_ref[k] = jnp.broadcast_to((g[:, k : k + 1] - n) * SCALE, (LANES, LANES))
    right_ref[...] = norms.T[:lines]
    found = reduced_over(
        lambda a, b: pairs_ref[b, a] > 0,
        4, 2,
        lambda k: tgt_ref[k].reshape(LANES, DL),
        lambda b: src_ref[pl.ds(b * 8, 8)].reshape(BLK, DL),
        bias_ref, score_ref, peak_ref, total_ref,
    )
    for k, line in enumerate(found):
        line_ref[k : k + 1] = line
    out_ref[...] = jnp.broadcast_to(line_ref[...][None], out_ref.shape)


def col_kernel(log2_nt, log2_ns, pairs_ref, src_ref, tgt_ref, got_ref,
               out_ref, f_ref,
               bias_ref, score_ref, peak_ref, total_ref):
    u = joined(got_ref[...])
    lines = u.shape[0]
    ut = turned(u)
    lane = lax.broadcasted_iota(jnp.int32, (LANES, LANES), 1)
    norms = jnp.zeros((LANES, LANES), f32)
    for k in range(lines):
        n = half_norms(src_ref[2 * k : 2 * k + 2].reshape(LANES, DL))
        norms = jnp.where(lane == k, n, norms)
        bias_ref[k] = jnp.broadcast_to((log2_nt - log2_ns) - ut[:, k : k + 1], (LANES, LANES))
    f_ref[...] = norms.T[:lines] + UNSCALE * (log2_nt - u)
    found = reduced_over(
        lambda a, b: pairs_ref[a, b] > 0,
        2, 4,
        lambda k: src_ref[pl.ds(2 * k, 2)].reshape(LANES, DL),
        lambda b: tgt_ref[pl.ds(b * 4, 4)].reshape(BLK, DL),
        bias_ref, score_ref, peak_ref, total_ref,
    )
    for k, line in enumerate(found):
        out_ref[k : k + 1] = line


def spread_kernel(got_ref, out_ref):
    out_ref[...] = jnp.broadcast_to(joined(got_ref[...])[None], out_ref.shape)


def last_kernel(got_ref, right_ref, g_ref):
    g_ref[...] = right_ref[...] - UNSCALE * joined(got_ref[...])


def shape(*dims, dtype=f32):
    return jax.ShapeDtypeStruct(dims, dtype)


def local(source, target, g_init, pairs):
    cols, zs = lax.axis_size("col"), lax.axis_size("z")
    sources = lax.all_to_all(
        jnp.broadcast_to(source[None], (cols, *source.shape)), "col", 0, 0, tiled=True
    )
    own = lax.all_gather(target, "z")
    other = lax.ppermute(own, "core", [(0, 1), (1, 0)])
    core = lax.axis_index("core").astype(jnp.int32).reshape(1)
    rows_dev = sources.shape[0] * sources.shape[1]
    cols_dev = 2 * own.shape[0] * own.shape[1]
    log2_nt = math.log2(cols * cols_dev)
    log2_ns = math.log2(zs * 2 * rows_dev)
    rl, cl = rows_dev // LANES, cols_dev // LANES
    rb, cb = pairs.shape
    scratch = lambda few, lines: [
        pltpu.VMEM((lines, LANES, LANES), f32),
        pltpu.VMEM((rb * cb, BLK // LANES, LANES, BLK), f32),
        pltpu.VMEM((few, 8, BLK), f32),
        pltpu.VMEM((few, 8, BLK), f32),
    ]
    spread, targets, right = pl.pallas_call(
        row_kernel,
        out_shape=(shape(cols, rl, LANES), shape(zs, 2, *target.shape, dtype=target.dtype), shape(cl, LANES)),
        in_specs=[SMEM, SMEM, VMEM, VMEM, VMEM, VMEM],
        out_specs=(VMEM, VMEM, VMEM),
        scratch_shapes=[pltpu.VMEM((rl, LANES), f32)] + scratch(rb, cl),
        compiler_params=pltpu.CompilerParams(vmem_limit_bytes=24 << 20),
        name="row_pass",
    )(pairs, core, sources, own, other, g_init.reshape(cl, LANES))
    got = lax.all_to_all(spread, "col", 0, 0, tiled=True)
    partial, f = pl.pallas_call(
        lambda *refs: col_kernel(log2_nt, log2_ns, *refs),
        out_shape=(shape(cl, LANES), shape(rl, LANES)),
        in_specs=[SMEM, VMEM, VMEM, VMEM],
        out_specs=(VMEM, VMEM),
        scratch_shapes=scratch(cb, rl),
        compiler_params=pltpu.CompilerParams(vmem_limit_bytes=24 << 20),
        name="col_pass",
    )(pairs, sources, targets, got)
    both = lax.all_gather(partial, "core")
    spread = pl.pallas_call(
        spread_kernel,
        out_shape=shape(zs, cl, LANES),
        in_specs=[VMEM],
        out_specs=VMEM,
        compiler_params=pltpu.CompilerParams(vmem_limit_bytes=4 << 20),
        name="spread",
    )(both)
    got = lax.all_to_all(spread, "z", 0, 0, tiled=True)
    g = pl.pallas_call(
        last_kernel,
        out_shape=shape(cl, LANES),
        in_specs=[VMEM, VMEM],
        out_specs=VMEM,
        compiler_params=pltpu.CompilerParams(vmem_limit_bytes=4 << 20),
        name="last",
    )(got, right)
    return (f.reshape(rows_dev), g.reshape(cols_dev))


def solution(mesh):
    finer = Mesh(mesh.devices.reshape(-1, 2, mesh.shape["col"]), ("z", "core", "col"))
    placed = (P(("z", "core", "col"), None), P(("col", "z", "core"), None), P("col"), P(ROW, "col"))
    return jax.shard_map(
        local, mesh=finer, in_specs=placed, out_specs=(P(ROW), P("col")), check_vma=False
    )
```

time: 153 us -> 108 us (0.71)
  the two profiles are of different devices: /device:TPU:1 before, /device:TPU:6 now
where the time goes in v1:
time: 108 us
  blocking collectives  75.1 us (70%)
  Pallas kernels  11.1 us (10%)
  waiting for transfers between devices  10 us (9%)
  starting transfers between devices  9.34 us (9%)
  local copies, waits for them, and re-layouts  1.52 us (1%)
    all_gather x1, blocking collectives, local(): own = lax.all_gather(target, 'z')  38.8 us
    all_to_all x1, blocking collectives, local(): got = lax.all_to_all(spread, 'z', 0, 0, tiled=True)  22.3 us
    all_to_all x1, blocking collectives, local(): got = lax.all_to_all(spread, 'col', 0, 0, tiled=True)  12.2 us
    all_to_all x1, waiting for transfers between devices, local(): lax.all_to_all(jnp.broadcast_to(source[None], (cols, *source.shape)), 'co...  10 us
    all_to_all x1, starting transfers between devices, local(): lax.all_to_all(jnp.broadcast_to(source[None], (cols, *source.shape)), 'co...  7.43 us
    pallas_call x1, Pallas kernels, local(): pl.pallas_call(row_kernel, out_shape=(shape(cols, rl, LANES), shape(zs, 2...  5.75 us
    pallas_call x1, Pallas kernels, local(): pl.pallas_call(lambda *refs: col_kernel(log2_nt, log2_ns, *refs), out_sha...  4.67 us
  transfers between devices with their start and end apart: 2, of which 1 were waited for; matrix products, arithmetic and copies ran while one was open for 1% of the time, Pallas kernels for 0%

profile of v1, /device:TPU:6, one launch (start us, length us, event | category | flops | bytes accessed | tf_op | source)
XLA Modules:
  0.0 107.8 jit_solution(14979889261012918944)
XLA Ops:
  0.6 0.0 copy-start.2
  0.6 38.8 %all-gather = bf16[1024,256]{1,0:T(8,128)(2,1)S(1)} all-gather(bf16[64,256]{1,0:T(8,128)(2,1)} %param.5), channel_id=2, replica_groups=mesh['z'=16,'core'=2,'col'=16] {'z'}, dimensions={0}, use_global_device_ids=true | all-gather | bytes 557056 | tf_op jit(solution)/shard_map/all_gather | solution.py:161
  39.4 1.9 %collective-permute-start = (bf16[16,64,256]{2,1,0:T(8,128)(2,1)S(1)}, bf16[16,64,256]{2,1,0:T(8,128)(2,1)S(1)}, u32[]{:S(2)}, u32[]{:S(2)}) collective-permute-start(bf16[16,64,256]{2,1,0:T(8,128)(2,1)S(1)} %bitcast.6), channel_id=1, source_target_pairs={{0,16},{16,0},{1,17},{17,1},{2,18},{18,2},{3,19},{19,3},{4,20},{20... | collective-permute-start | bytes 1572872 | tf_op jit(solution)/shard_map/ppermute | solution.py:162
  41.4 0.0 copy-done.2
  41.4 0.8 broadcast_in_dim.2
  42.2 7.4 %all-to-all-start = ((bf16[16,64,256]{2,1,0:T(8,128)(2,1)}), bf16[16,64,256]{2,1,0:T(8,128)(2,1)S(1)}, u32[]{:S(2)}, u32[]{:S(2)}) async-start(bf16[16,64,256]{2,1,0:T(8,128)(2,1)} %broadcast_in_dim.2), calls=%async_computation | async-start | bytes 1048576 | tf_op jit(solution)/shard_map/all_to_all | solution.py:158
  49.6 0.0 copy-start
  49.6 10.0 %all-to-all-done.src_ref.refs_1_ = bf16[16,64,256]{2,1,0:T(8,128)(2,1)S(1)} async-done(((bf16[16,64,256]{2,1,0:T(8,128)(2,1)}), bf16[16,64,256]{2,1,0:T(8,128)(2,1)S(1)}, u32[]{:S(2)}, u32[]{:S(2)}) %all-to-all-start) | async-done | bytes 524320 | tf_op jit(solution)/shard_map/all_to_all | solution.py:158
  59.7 0.0 collective-permute-done.other_ref
  59.7 0.0 copy-start.1
  59.7 0.0 copy-done
  59.7 0.7 copy-done.1
  60.3 5.8 %row_pass.1 = (f32[16,8,128]{2,1,0:T(8,128)S(1)}, bf16[16,2,64,256]{3,2,1,0:T(8,128)(2,1)S(1)}, f32[16,128]{1,0:T(8,128)S(1)}) custom-call(s32[2,4]{1,0:T(2,128)S(1)} %copy-done.1, s32[1]{0:T(128)} %bitcast.core_ref, bf16[16,64,256]{2,1,0:T(8,128)(2,1)S(1)} %all-to-all-done.src_ref.refs_1_, bf16[16,64,256]{2,1,0:T(8,128)(2,1)S(1)} %bitcast.7, ...), custom_call_target="tpu_custom_call" | custom-call | tf_op jit(solution)/shard_map/row_pass/pallas_call | solution.py:176
  66.1 12.2 %all_to_all.15.refs_3_ = f32[16,8,128]{2,1,0:T(8,128)S(1)} all-to-all(f32[16,8,128]{2,1,0:T(8,128)S(1)} %get-tuple-element.8), channel_id=1, replica_groups=mesh['z'=16,'core'=2,'col'=16] {'col'}, dimensions={0} | all-to-all | bytes 131072 | tf_op jit(solution)/shard_map/all_to_all | solution.py:185
  78.3 4.7 %col_pass.1 = (f32[16,128]{1,0:T(8,128)S(1)}, f32[8,128]{1,0:T(8,128)}) custom-call(s32[2,4]{1,0:T(2,128)S(1)} %copy-done.1, bf16[16,64,256]{2,1,0:T(8,128)(2,1)S(1)} %all-to-all-done.src_ref.refs_1_, bf16[16,2,64,256]{3,2,1,0:T(8,128)(2,1)S(1)} %get-tuple-element.7.refs_2_, f32[16,8,128]{2,1,0:T(8,128)S(1)} %all_to_all.15.refs_3_), custom_call_target="tpu_custom_call" | custom-call | tf_op jit(solution)/shard_map/col_pass/pallas_call | solution.py:186
  82.9 1.8 %all-gather.1 = f32[32,128]{1,0:T(8,128)S(1)} all-gather(f32[16,128]{1,0:T(8,128)S(1)} %get-tuple-element.10), channel_id=3, replica_groups=mesh['z'=16,'core'=2,'col'=16] {'core'}, dimensions={0}, use_global_device_ids=true | all-gather | bytes 24576 | tf_op jit(solution)/shard_map/all_gather | solution.py:195
  84.8 22.3 %all_to_all.16.got_ref = f32[16,16,128]{2,1,0:T(8,128)S(1)} all-to-all(f32[16,16,128]{2,1,0:T(8,128)S(1)} %spread.1), channel_id=1, replica_groups=mesh['z'=16,'core'=2,'col'=16] {'z'}, dimensions={0} | all-to-all | bytes 262144 | tf_op jit(solution)/shard_map/all_to_all | solution.py:204
  107.1 0.6 last.1
  (1 shorter events, 0.0 us)
Async XLA Ops:
  0.6 40.7 %copy-start.2 = (bf16[64,256]{1,0:T(8,128)(2,1)S(1)}, bf16[64,256]{1,0:T(8,128)(2,1)}, u32[]{:S(2)}) copy-start(bf16[64,256]{1,0:T(8,128)(2,1)} %param.4) | copy-start | bytes 98308
  39.4 20.2 %collective-permute-start = (bf16[16,64,256]{2,1,0:T(8,128)(2,1)S(1)}, bf16[16,64,256]{2,1,0:T(8,128)(2,1)S(1)}, u32[]{:S(2)}, u32[]{:S(2)}) collective-permute-start(bf16[16,64,256]{2,1,0:T(8,128)(2,1)S(1)} %bitcast.6), channel_id=1, source_target_pairs={{0,16},{16,0},{1,17},{17,1},{2,18},{18,2},{3,19},{19,3},{4,20},{20... | collective-permute-start | bytes 1572872 | tf_op jit(solution)/shard_map/ppermute | solution.py:162
  42.2 17.4 %all-to-all-start = ((bf16[16,64,256]{2,1,0:T(8,128)(2,1)}), bf16[16,64,256]{2,1,0:T(8,128)(2,1)S(1)}, u32[]{:S(2)}, u32[]{:S(2)}) async-start(bf16[16,64,256]{2,1,0:T(8,128)(2,1)} %broadcast_in_dim.2), calls=%async_computation | async-start | bytes 1048576 | tf_op jit(solution)/shard_map/all_to_all | solution.py:158
  49.6 10.0 %copy-start = (f32[2048]{0:T(1024)S(1)}, f32[2048]{0:T(1024)}, u32[]{:S(2)}) copy-start(f32[2048]{0:T(1024)} %param.6) | copy-start | bytes 24580
  59.7 0.7 copy-start.1

commit v2 on v1

v2 whole, which is shorter than its diff:
```python
import math

import jax
import jax.numpy as jnp
from jax import lax
from jax.experimental import pallas as pl
from jax.experimental.pallas import tpu as pltpu
from jax.sharding import Mesh
from jax.sharding import PartitionSpec as P


BLK = 512
DL = 256
LANES = 128
SUB = 8
EPSILON = 0.1
VERY_LOW = -1e30
SCALE = 1.0 / EPSILON
ROW = ("z", "core")
VMEM = pl.BlockSpec(memory_space=pltpu.VMEM)
SMEM = pl.BlockSpec(memory_space=pltpu.SMEM)
f32 = jnp.float32


def half_norms(x):
    x = x.astype(f32)
    return 0.5 * jnp.sum(x * x, axis=1, keepdims=True)


def dot(x, y):
    return lax.dot_general(x, y, (((1,), (1,)), ((), ())), preferred_element_type=f32)


def turned(x):
    rows = x.shape[0]
    if rows < LANES:
        x = jnp.concatenate([x, jnp.zeros((LANES - rows, LANES), f32)], axis=0)
    return x.T


def wide(x, times):
    return jnp.concatenate([x] * times, axis=1)


def joined(parts):
    peak = jnp.max(parts, axis=0)
    return peak + jnp.log(jnp.sum(jnp.exp(parts - peak[None]), axis=0))


def added(state, s):
    s = s.reshape(s.shape[0] // SUB, SUB, s.shape[1])
    peak = jnp.max(s, axis=0)
    if state is not None:
        peak = jnp.maximum(peak, state[0])
    total = jnp.sum(jnp.exp(s - peak[None]), axis=0)
    if state is not None:
        total = total + state[1] * jnp.exp(state[0] - peak)
    return peak, total


def closed(peak, total):
    top = jnp.max(peak, axis=0, keepdims=True)
    total = jnp.sum(total * jnp.exp(peak - top), axis=0, keepdims=True)
    return jnp.where(top > 0.5 * VERY_LOW, top + jnp.log(total), VERY_LOW)


def fan_kernel(x_ref, out_ref):
    out_ref[...] = jnp.broadcast_to(x_ref[...][None], out_ref.shape)


def keep_bias(pairs_ref, rb, cb):
    return jnp.where(pairs_ref[rb, cb] > 0, 0.0, VERY_LOW)


def piece_kernel(index, *refs):
    last = index == 1
    pairs_ref, place_ref, q_ref, g_ref, src_ref = refs[:5]
    if last:
        peak_in, total_in, _, norm_in, out_ref, right_ref, tgt_ref, bias_ref, turn_ref, line_ref = refs[5:]
    else:
        peak_ref, total_ref, tgt_ref, norm_ref, bias_ref, turn_ref = refs[5:]
    place = place_ref[0]
    group = (place + place // 2 + index) % 2
    chips = q_ref.shape[0]
    lane = lax.broadcasted_iota(jnp.int32, (64, LANES), 1)
    norms = jnp.zeros((64, LANES), f32)
    turn_ref[...] = turned(g_ref[...])
    for z in range(chips):
        core = (group + z) % 2
        g = turn_ref[pl.ds(pl.multiple_of(core * 64, 64), 64), :]
        x = q_ref[z]
        tgt_ref[z, core] = x
        n = half_norms(x)
        norms = jnp.where(lane == z, n, norms)
        bias_ref[z] = jnp.broadcast_to((g[:, z : z + 1] - n) * SCALE, (64, LANES))
    per = 2
    lines = []
    for rb in range(pairs_ref.shape[0]):
        y = src_ref[rb * 8 : rb * 8 + 8].reshape(BLK, DL)
        state = (peak_in[rb], total_in[rb]) if last else None
        for c in range(0, chips, per):
            x = q_ref[c : c + per].reshape(per * 64, DL)
            bias = bias_ref[c : c + per].reshape(per * 64, LANES) + keep_bias(pairs_ref, rb, c // 4)
            state = added(state, dot(x, y) * SCALE + wide(bias, BLK // LANES))
        if last:
            line = closed(*state)
            lines += [line[:, k * LANES : (k + 1) * LANES] for k in range(BLK // LANES)]
        else:
            peak_ref[rb], total_ref[rb] = state
    if last:
        for k, line in enumerate(lines):
            line_ref[k : k + 1] = line
        out_ref[...] = jnp.broadcast_to(line_ref[...][None], out_ref.shape)
        swapped = (lane + group) % 2 == 0
        first, second = jnp.where(swapped, norms, norm_in[...]), jnp.where(swapped, norm_in[...], norms)
        right_ref[...] = jnp.concatenate([first, second], axis=0).T[:chips]
    else:
        norm_ref[...] = norms


def col_kernel(log_nt, log_ns, pairs_ref, src_ref, tgt_ref, got_ref, out_ref, f_ref, bias_ref):
    u = joined(got_ref[...])
    lines = u.shape[0]
    ut = turned((log_nt - log_ns) - u)
    lane = lax.broadcasted_iota(jnp.int32, (LANES, LANES), 1)
    norms = jnp.zeros((LANES, LANES), f32)
    for k in range(lines):
        n = half_norms(src_ref[2 * k : 2 * k + 2].reshape(LANES, DL))
        norms = jnp.where(lane == k, n, norms)
        bias_ref[k] = jnp.broadcast_to(ut[:, k : k + 1], (LANES, LANES))
    f_ref[...] = norms.T[:lines] + EPSILON * (log_nt - u)
    _, cbs = pairs_ref.shape
    for b in range(cbs):
        y = tgt_ref[b * 4 : b * 4 + 4].reshape(BLK, DL)
        state = None
        for k in range(lines):
            x = src_ref[2 * k : 2 * k + 2].reshape(LANES, DL)
            bias = bias_ref[k] + keep_bias(pairs_ref, k * LANES // BLK, b)
            state = added(state, dot(x, y) * SCALE + wide(bias, BLK // LANES))
        line = closed(*state)
        for k in range(BLK // LANES):
            out_ref[4 * b + k : 4 * b + k + 1] = line[:, k * LANES : (k + 1) * LANES]


def spread_kernel(got_ref, out_ref):
    out_ref[...] = jnp.broadcast_to(joined(got_ref[...])[None], out_ref.shape)


def last_kernel(got_ref, right_ref, g_ref):
    g_ref[...] = right_ref[...] - EPSILON * joined(got_ref[...])


def shape(*dims, dtype=f32):
    return jax.ShapeDtypeStruct(dims, dtype)


def kernel_call(body, outs, ins, mib=8, scratch=(), aliases={}, flops=0, bytes_accessed=0):
    single = not isinstance(outs, tuple)
    return pl.pallas_call(
        body,
        out_shape=outs,
        in_specs=ins,
        out_specs=VMEM if single else (VMEM,) * len(outs),
        scratch_shapes=list(scratch),
        input_output_aliases=aliases,
        compiler_params=pltpu.CompilerParams(vmem_limit_bytes=mib << 20),
        cost_estimate=pl.CostEstimate(flops=flops, bytes_accessed=bytes_accessed, transcendentals=0),
    )


def local(source, target, g_init, pairs):
    cols, zs = lax.axis_size("col"), lax.axis_size("z")
    rows_dev, cols_dev = cols * source.shape[0], 2 * zs * target.shape[0]
    log_nt, log_ns = math.log(cols * cols_dev), math.log(zs * 2 * rows_dev)
    rl, cl = rows_dev // LANES, cols_dev // LANES
    rb, _ = pairs.shape
    alternating = [[2 * z + (z + group) % 2 for z in range(zs)] for group in range(2)]

    fanned = kernel_call(fan_kernel, shape(cols, *source.shape, dtype=source.dtype), [VMEM], mib=2)(source)
    sources = lax.all_to_all(fanned, "col", 0, 0, tiled=True)
    g_lines = g_init.reshape(cl, LANES)
    near = lax.all_gather(target, ROW, axis_index_groups=alternating)
    other = lax.ppermute(near, "core", [(0, 1), (1, 0)])
    place = lax.axis_index(ROW).astype(jnp.int32).reshape(1)

    kept = shape(zs, 2, *target.shape, dtype=target.dtype)
    bias = [pltpu.VMEM((zs, 64, LANES), f32), pltpu.VMEM((LANES, LANES), f32)]
    state = (shape(rb, SUB, BLK),) * 2
    work = dict(flops=cols_dev * rows_dev * DL, bytes_accessed=1 << 20)
    state = kernel_call(
        lambda *refs: piece_kernel(0, *refs),
        (*state, kept, shape(64, LANES)),
        [SMEM, SMEM, VMEM, VMEM, VMEM], scratch=bias, **work,
    )(pairs, place, near, g_lines, sources)
    sent, right, targets = kernel_call(
        lambda *refs: piece_kernel(1, *refs),
        (shape(cols, rl, LANES), shape(cl, LANES), kept),
        [SMEM, SMEM] + [VMEM] * 7, scratch=[*bias, pltpu.VMEM((rl, LANES), f32)], aliases={7: 2}, **work,
    )(pairs, place, other, g_lines, sources, *state)
    got = lax.all_to_all(sent, "col", 0, 0, tiled=True)
    partial, f = kernel_call(
        lambda *refs: col_kernel(log_nt, log_ns, *refs),
        (shape(cl, LANES), shape(rl, LANES)),
        [SMEM, VMEM, VMEM, VMEM], scratch=[pltpu.VMEM((rl, LANES, LANES), f32)],
    )(pairs, sources, targets, got)
    both = lax.all_gather(partial, "core")
    sent = kernel_call(spread_kernel, shape(zs, cl, LANES), [VMEM], mib=4)(both)
    got = lax.all_to_all(sent, "z", 0, 0, tiled=True)
    g = kernel_call(last_kernel, shape(cl, LANES), [VMEM, VMEM], mib=4)(got, right)
    return (f.reshape(rows_dev), g.reshape(cols_dev))


def solution(mesh):
    finer = Mesh(mesh.devices.reshape(-1, 2, mesh.shape["col"]), (*ROW, "col"))
    placed = (P((*ROW, "col"), None), P(("col", *ROW), None), P("col"), P(ROW, "col"))
    return jax.shard_map(local, mesh=finer, in_specs=placed, out_specs=(P(ROW), P("col")), check_vma=False)
```

time: 108 us -> 95.8 us (0.89)
  the two profiles are of different devices: /device:TPU:6 before, /device:TPU:1 now
where the time goes in v2:
time: 95.8 us; the launch traced here: 94.4 us
  blocking collectives  70.6 us (74%)
  Pallas kernels  11.9 us (12%)
  starting transfers between devices  9.72 us (10%)
  local copies, waits for them, and re-layouts  1.43 us (1%)
    all_gather x1, blocking collectives, local(): near = lax.all_gather(target, ROW, axis_index_groups=alternating)  35.8 us
    all_to_all x1, blocking collectives, local(): got = lax.all_to_all(sent, 'z', 0, 0, tiled=True)  18.3 us
    all_to_all x1, blocking collectives, local(): got = lax.all_to_all(sent, 'col', 0, 0, tiled=True)  13.2 us
    all_to_all x1, starting transfers between devices, local(): sources = lax.all_to_all(fanned, 'col', 0, 0, tiled=True)  7.7 us
    pallas_call x1, Pallas kernels, local(): kernel_call(lambda *refs: col_kernel(log_nt, log_ns, *refs), (shape(cl, L...  4.54 us
    all_gather x1, blocking collectives, local(): both = lax.all_gather(partial, 'core')  3.28 us
    pallas_call x1, Pallas kernels, local(): kernel_call(lambda *refs: piece_kernel(1, *refs), (shape(cols, rl, LANES)...  2.97 us
    pallas_call x1, Pallas kernels, local(): kernel_call(lambda *refs: piece_kernel(0, *refs), (*state, kept, shape(64...  2.88 us
  transfers between devices with their start and end apart: 2, of which 0 were waited for; matrix products, arithmetic and copies ran while one was open for 0% of the time, Pallas kernels for 3%

profile of v2, /device:TPU:1, one launch (start us, length us, event | category | flops | bytes accessed | tf_op | source)
XLA Modules:
  0.0 94.4 jit_solution(10899650710001255954)
XLA Ops:
  0.6 0.0 copy-start
  0.6 0.7 copy-done
  1.4 0.8 shard_map.59
  2.2 0.0 copy-start.3
  2.2 7.7 %all-to-all-start = ((bf16[16,64,256]{2,1,0:T(8,128)(2,1)}), bf16[16,64,256]{2,1,0:T(8,128)(2,1)S(1)}, u32[]{:S(2)}, u32[]{:S(2)}) async-start(bf16[16,64,256]{2,1,0:T(8,128)(2,1)} %shard_map.59), calls=%async_computation | async-start | bytes 1048576 | tf_op jit(solution)/shard_map/all_to_all | solution.py:180
  10.0 0.0 copy-done.3
  10.0 35.8 %all-gather = bf16[1024,256]{1,0:T(8,128)(2,1)S(1)} all-gather(bf16[64,256]{1,0:T(8,128)(2,1)S(1)} %copy-done.3), channel_id=2, replica_groups={{0,48,64,112,128,176,192,240,256,304,320,368,384,432,448,496},{16,32,80..., dimensions={0}, use_global_device_ids=true | all-gather | bytes 557056 | tf_op jit(solution)/shard_map/all_gather | solution.py:182
  45.8 2.0 %collective-permute-start = (bf16[16,64,256]{2,1,0:T(8,128)(2,1)S(1)}, bf16[16,64,256]{2,1,0:T(8,128)(2,1)S(1)}, u32[]{:S(2)}, u32[]{:S(2)}) collective-permute-start(bf16[16,64,256]{2,1,0:T(8,128)(2,1)S(1)} %bitcast.6), channel_id=1, source_target_pairs={{0,16},{16,0},{1,17},{17,1},{2,18},{18,2},{3,19},{19,3},{4,20},{20... | collective-permute-start | bytes 1572872 | tf_op jit(solution)/shard_map/ppermute | solution.py:183
  47.8 0.0 copy-start.1
  47.8 0.0 all-to-all-done.refs_4_.refs_1_
  47.8 0.0 copy-start.2
  47.8 0.7 copy-done.1
  48.5 0.0 copy-done.2
  48.5 2.9 %shard_map.60 = (f32[2,8,512]{2,1,0:T(8,128)S(1)}, f32[2,8,512]{2,1,0:T(8,128)S(1)}, bf16[16,2,64,256]{3,2,1,0:T(8,128)(2,1)S(1)}, f32[64,128]{1,0:T(8,128)S(1)}) custom-call(s32[2,4]{1,0:T(2,128)S(1)} %copy-done.2, s32[1]{0:T(128)} %bitcast.refs_1_, bf16[16,64,256]{2,1,0:T(8,128)(2,1)S(1)} %bitcast.7, f32[16,128]{1,0:T(8,128)S(1)} %bitcast.9, ...), custom_call_target="tpu_custom_call" | custom-call | flops 536870912 | bytes 1048576 | tf_op jit(solution)/shard_map/pallas_call | solution.py:190
  51.4 0.0 collective-permute-done.refs_2_
  51.4 3.0 %shard_map.61 = (f32[16,8,128]{2,1,0:T(8,128)S(1)}, f32[16,128]{1,0:T(8,128)S(1)}, bf16[16,2,64,256]{3,2,1,0:T(8,128)(2,1)S(1)}) custom-call(s32[2,4]{1,0:T(2,128)S(1)} %copy-done.2, s32[1]{0:T(128)} %bitcast.refs_1_, bf16[16,64,256]{2,1,0:T(8,128)(2,1)S(1)} %collective-permute-done.refs_2_, ...), custom_call_target="tpu_custom_call", output_to_operand_aliasing={{2}: (7, {})} | custom-call | flops 536870912 | bytes 1048576 | tf_op jit(solution)/shard_map/pallas_call | solution.py:195
  54.4 13.2 %all_to_all.15.refs_3_ = f32[16,8,128]{2,1,0:T(8,128)S(1)} all-to-all(f32[16,8,128]{2,1,0:T(8,128)S(1)} %get-tuple-element.16), channel_id=1, replica_groups=mesh['z'=16,'core'=2,'col'=16] {'col'}, dimensions={0} | all-to-all | bytes 131072 | tf_op jit(solution)/shard_map/all_to_all | solution.py:200
  67.6 4.5 %shard_map.62 = (f32[16,128]{1,0:T(8,128)S(1)}, f32[8,128]{1,0:T(8,128)}) custom-call(s32[2,4]{1,0:T(2,128)S(1)} %copy-done.2, bf16[16,64,256]{2,1,0:T(8,128)(2,1)S(1)} %all-to-all-done.refs_4_.refs_1_, bf16[16,2,64,256]{3,2,1,0:T(8,128)(2,1)S(1)} %get-tuple-element.15.refs_2_, f32[16,8,128]{2,1,0:T(8,128)S(1)} %all_to_all.15.refs_3_), custom_call_target="tpu_custom_call" | custom-call | tf_op jit(solution)/shard_map/pallas_call | solution.py:201
  72.1 3.3 %all-gather.1 = f32[32,128]{1,0:T(8,128)S(1)} all-gather(f32[16,128]{1,0:T(8,128)S(1)} %get-tuple-element.18), channel_id=3, replica_groups=mesh['z'=16,'core'=2,'col'=16] {'core'}, dimensions={0}, use_global_device_ids=true | all-gather | bytes 24576 | tf_op jit(solution)/shard_map/all_gather | solution.py:206
  75.4 18.3 %all_to_all.16.got_ref = f32[16,16,128]{2,1,0:T(8,128)S(1)} all-to-all(f32[16,16,128]{2,1,0:T(8,128)S(1)} %shard_map.63), channel_id=1, replica_groups=mesh['z'=16,'core'=2,'col'=16] {'z'}, dimensions={0} | all-to-all | bytes 262144 | tf_op jit(solution)/shard_map/all_to_all | solution.py:208
  93.8 0.6 shard_map.64
  (1 shorter events, 0.0 us)
Async XLA Ops:
  0.6 0.8 copy-start
  2.2 7.7 %copy-start.3 = (bf16[64,256]{1,0:T(8,128)(2,1)S(1)}, bf16[64,256]{1,0:T(8,128)(2,1)}, u32[]{:S(2)}) copy-start(bf16[64,256]{1,0:T(8,128)(2,1)} %param.5) | copy-start | bytes 98308
  2.2 45.6 %all-to-all-start = ((bf16[16,64,256]{2,1,0:T(8,128)(2,1)}), bf16[16,64,256]{2,1,0:T(8,128)(2,1)S(1)}, u32[]{:S(2)}, u32[]{:S(2)}) async-start(bf16[16,64,256]{2,1,0:T(8,128)(2,1)} %shard_map.59), calls=%async_computation | async-start | bytes 1048576 | tf_op jit(solution)/shard_map/all_to_all | solution.py:180
  45.8 5.6 %collective-permute-start = (bf16[16,64,256]{2,1,0:T(8,128)(2,1)S(1)}, bf16[16,64,256]{2,1,0:T(8,128)(2,1)S(1)}, u32[]{:S(2)}, u32[]{:S(2)}) collective-permute-start(bf16[16,64,256]{2,1,0:T(8,128)(2,1)S(1)} %bitcast.6), channel_id=1, source_target_pairs={{0,16},{16,0},{1,17},{17,1},{2,18},{18,2},{3,19},{19,3},{4,20},{20... | collective-permute-start | bytes 1572872 | tf_op jit(solution)/shard_map/ppermute | solution.py:183
  47.8 0.7 copy-start.1
  47.8 0.7 copy-start.2
